TPU v7x, 32 devices: a whole 2x2x4 slice. The times are simulated.
32 devices in a mesh: member: 2 (over core), shard: 16 (over z, y, x).
Axes of the slice: x: 2, y: 2, z: 4, core: 2. Of those that a mesh axis runs over, the one named last changes fastest.
Arguments:
- layer_input: bfloat16 [2, 180, 5120], P('member', None, 'shard'), may hold values from -6 to 6
- norm_gain: float32 [2, 5120], P('member'), may hold values from 0.5 to 2
- w_gate: bfloat16 [2, 5120, 1792], P('member', None, 'shard'), may hold values from -0.0559017 to 0.0559017
- w_up: bfloat16 [2, 5120, 1792], P('member', None, 'shard'), may hold values from -0.0559017 to 0.0559017
- hidden_cot: bfloat16 [2, 180, 1792], P('member', None, 'shard'), may hold values from -3 to 5
- output_cot: bfloat16 [2, 180, 5120], P('member', None, 'shard'), may hold values from -6 to 6
- embed: bfloat16 [2, 4096, 5120], P('member', 'shard'), may hold values from -0.078125 to 0.078125
- suffix_ids: int32 [180], replicated, may hold values from 0 to 4095
Outputs:
- delta: float32 [180, 4096], P(None, 'shard')
All inputs are finite; a program needn't handle non-finite values.
Results may differ from a plain program's by a relative error of at most 0.0047.
Values may be sent and summed in bfloat16 or wider, within the bound.
A program may use at most 64 MiB of HBM per device.

v0:
```python
import jax
import jax.numpy as jnp
from jax import lax
from jax.sharding import PartitionSpec as P


def on_device(layer_input, norm_gain, w_gate, w_up, hidden_cot, output_cot, embed, suffix_ids):
    input_local = layer_input[0]
    cot_local = output_cot[0]
    gain = norm_gain[0]
    gate_w = w_gate[0]
    up_w = w_up[0]
    table = embed[0]
    whole_input = lax.all_gather(input_local, "shard", axis=1, tiled=True)
    inputs = whole_input.astype(jnp.float32)
    width = inputs.shape[1]
    inv_rms = 1.0 / jnp.sqrt(jnp.mean(inputs * inputs, axis=1, keepdims=True) + 1e-05)
    normed = (inputs * inv_rms * gain[None, :]).astype(jnp.bfloat16)
    gate_pre = jnp.dot(normed, gate_w, preferred_element_type=jnp.float32)
    up_proj = jnp.dot(normed, up_w, preferred_element_type=jnp.float32)
    sigmoid_gate = jax.nn.sigmoid(gate_pre)
    hid_f = hidden_cot[0].astype(jnp.float32)
    gate_grad = (hid_f * up_proj * sigmoid_gate * (1.0 + gate_pre * (1.0 - sigmoid_gate))).astype(
        jnp.bfloat16
    )
    up_grad = (hid_f * gate_pre * sigmoid_gate).astype(jnp.bfloat16)
    contract = (((1,), (1,)), ((), ()))
    share_width = input_local.shape[1]
    part = lax.dot_general(gate_w, gate_grad, contract, preferred_element_type=jnp.float32)
    share_t = lax.psum_scatter(
        part + lax.dot_general(up_w, up_grad, contract, preferred_element_type=jnp.float32),
        "shard",
        scatter_dimension=0,
        tiled=True,
    )
    share = share_t.T
    offset = lax.axis_index("shard") * share_width
    gain_share = lax.dynamic_slice_in_dim(gain, offset, share_width, 0)
    input_share = input_local.astype(jnp.float32)
    scaled = share * gain_share[None, :]
    partial_proj = jnp.sum(input_share * scaled, axis=1)
    proj = lax.psum(partial_proj, "shard")[:, None] / width
    grad_share = cot_local.astype(jnp.float32) + inv_rms * scaled - input_share * inv_rms**3 * proj
    grad_share = grad_share.astype(jnp.bfloat16)
    scores = lax.dot_general(
        lax.all_gather(grad_share, "shard", axis=1, tiled=True),
        table,
        contract,
        preferred_element_type=jnp.float32,
    )
    vocab_local = table.shape[0]
    first_entry = lax.axis_index("shard") * vocab_local
    entries = first_entry + lax.broadcasted_iota(jnp.int32, (1, vocab_local), 1)
    own_mask = (suffix_ids[:, None] == entries).astype(jnp.float32)
    own_local = jnp.sum(scores * own_mask, axis=1)
    current = lax.psum(own_local, "shard")
    delta = lax.psum(scores - current[:, None], "member")
    return delta


def solution(mesh):
    placed = (
        P("member", None, "shard"),
        P("member", None),
        P("member", None, "shard"),
        P("member", None, "shard"),
        P("member", None, "shard"),
        P("member", None, "shard"),
        P("member", "shard", None),
        P(),
    )
    return jax.shard_map(
        on_device, mesh=mesh, in_specs=placed, out_specs=P(None, "shard"), check_vma=False
    )
```

profile of v0, /device:TPU:0, one launch (start us, length us, event | category | flops | bytes accessed | tf_op | source)
XLA Modules:
  0.0 417.3 jit_solution(5285484548928964807)
XLA Ops:
  6.5 0.0 copy-start
  6.5 0.0 all-gather.5.cloned.1.call-start
  6.5 2.0 copy.12
  8.5 0.0 all-gather.5.cloned.1.call-update
  8.6 0.0 reduce-scatter.4.cloned.1.call-start
  8.6 88.6 %all-gather.5.cloned.1.call-done = bf16[1,180,5120]{1,0,2:T(2,128)(2,1)} async-done(((bf16[1,180,320]{1,0,2:T(2,128)(2,1)}), bf16[1,180,5120]{1,0,2:T(2,128)(2,1)}) %all-gather.5.cloned.1.call-update) | async-done | bytes 1843216 | tf_op jit(solution)/shard_map/all_gather | solution.py:14
  97.2 0.0 copy-start.5
  97.2 11.0 %copy.13 = bf16[1,180,5120]{2,1,0:T(8,128)(2,1)} copy(bf16[1,180,5120]{1,0,2:T(2,128)(2,1)} %all-gather.5.cloned.1.call-done) | data formatting | bytes 3686400 | tf_op jit(solution)/shard_map/all_gather | solution.py:14
  108.2 0.0 copy-start.1
  108.2 2.1 fusion.1
  110.3 0.0 copy-done.5
  110.3 0.0 copy-done.1
  110.3 0.0 copy-start.3
  110.3 2.1 fusion.8
  112.4 0.0 copy-done.3
  112.5 6.2 %fusion.6 = f32[180,5120]{1,0:T(8,128)} fusion(bf16[1,5120,112]{1,2,0:T(8,128)(2,1)} %param.10, bf16[1,5120,112]{1,2,0:T(8,128)(2,1)} %param.11, bf16[1,180,5120]{2,1,0:T(8,128)(2,1)} %copy.13, f32[5120]{0:T(1024)S(1)} %bitcast.68, f32[180]{0:T(256)S(1)} %get-tuple-element.6, f32[180,112]{1,0:T(8,128)S(1)} %fusion.8, bf16[1,180,112]{2,1,0:T(8,128)(2,1)S(1)} %copy-done.3), kind=kOutput, calls=%fused_computation.9 | convolution fusion | flops 416784960 | bytes 7965520 | tf_op jit(solution)/shard_map/dot_general | solution.py:29
  118.7 4.9 %fusion = f32[5120,180]{0,1:T(8,128)} fusion(f32[180,5120]{1,0:T(8,128)} %fusion.6, bf16[1,5120,112]{1,2,0:T(8,128)(2,1)} %param.11, f32[180,112]{1,0:T(8,128)S(1)} %fusion.8, bf16[1,180,112]{2,1,0:T(8,128)(2,1)S(1)} %copy-done.3), kind=kOutput, calls=%fused_computation.1 | convolution fusion | flops 207501120 | bytes 8640640 | tf_op jit(solution)/shard_map/dot_general | solution.py:31
  123.6 5.6 %copy.15 = f32[5120,180]{1,0:T(8,128)} copy(f32[5120,180]{0,1:T(8,128)} %fusion) | data formatting | bytes 7372800
  129.2 0.0 copy-start.2
  129.2 0.0 copy-start.4
  129.2 0.0 reduce-scatter.4.cloned.1.call-update
  129.3 0.0 all-gather.7.cloned.1.call-start
  129.3 0.1 dynamic-slice_reduce_fusion
  129.4 114.3 %reduce-scatter.4.cloned.1.call-done = f32[320,180]{1,0:T(8,128)} async-done(((f32[5120,180]{1,0:T(8,128)}), f32[320,180]{1,0:T(8,128)}) %reduce-scatter.4.cloned.1.call-update) | async-done | bytes 230416
  243.7 1.1 copy.16
  244.9 0.0 copy-done.2
  244.9 0.1 fusion.33
  245.0 41.3 %psum.21 = f32[180]{0:T(256)S(1)} all-reduce(f32[180]{0:T(256)S(1)} %fusion.33), channel_id=1, replica_groups=mesh['member'=2,'shard'=16] {'shard'}, use_global_device_ids=true, to_apply=%region_3.0 | all-reduce | flops 180 | bytes 1440 | tf_op jit(solution)/shard_map/psum | solution.py:42
  286.3 0.0 copy-done.4
  286.3 0.8 fusion.34
  287.1 0.0 all-gather.7.cloned.1.call-update
  287.1 0.0 all-reduce.2.cloned.1.call-start
  287.2 57.4 %all-gather.7.cloned.1.call-done = bf16[16,320,180]{1,2,0:T(8,128)(2,1)} async-done(((bf16[1,320,180]{1,2,0:T(8,128)(2,1)}), bf16[16,320,180]{1,2,0:T(8,128)(2,1)}) %all-gather.7.cloned.1.call-update) | async-done | bytes 1843216 | tf_op jit(solution)/shard_map/all_gather | solution.py:46
  344.6 3.3 copy.14
  347.9 0.0 copy-start.6
  347.9 4.5 %reshape.35 = bf16[5120,180]{0,1:T(8,128)(2,1)} reshape(bf16[16,320,180]{1,0,2:T(8,128)(2,1)} %copy.14) | data formatting | bytes 3686400
  352.5 0.0 copy-done
  352.5 0.0 copy-done.6
  352.5 2.6 select_reduce_fusion
  355.1 39.2 %psum.22 = f32[180]{0:T(256)S(1)} all-reduce(f32[180]{0:T(256)S(1)} %get-tuple-element.7), channel_id=1, replica_groups=mesh['member'=2,'shard'=16] {'shard'}, use_global_device_ids=true, to_apply=%region_5.0 | all-reduce | flops 180 | bytes 1440 | tf_op jit(solution)/shard_map/psum | solution.py:56
  394.3 0.8 broadcast_subtract_fusion
  395.1 0.0 all-reduce.2.cloned.1.call-update
  395.1 14.1 %all-reduce.2.cloned.1.call-done = f32[180,256]{1,0:T(8,128)} async-done(((f32[180,256]{1,0:T(8,128)}), f32[180,256]{1,0:T(8,128)}) %all-reduce.2.cloned.1.call-update) | async-done | bytes 184336 | tf_op jit(solution)/shard_map/psum | solution.py:57
  409.2 1.6 copy.18
  (3 shorter events, 0.0 us)
Async XLA Ops:
  6.5 345.9 %copy-start = (bf16[1,256,5120]{2,1,0:T(8,128)(2,1)S(1)}, bf16[1,256,5120]{2,1,0:T(8,128)(2,1)}, u32[]{:S(2)}) copy-start(bf16[1,256,5120]{2,1,0:T(8,128)(2,1)} %param.14) | copy-start | bytes 7864324
  6.5 90.6 %all-gather.5.cloned.1.call-start = ((), (), s32[]{:S(2)}) async-start(), calls=%async_computation.2 | async-start | bytes 5570560 | tf_op jit(solution)/shard_map/all_gather | solution.py:14
  8.6 235.2 %reduce-scatter.4.cloned.1.call-start = ((), (), s32[]{:S(2)}) async-start(), calls=%async_computation.4 | async-start | bytes 5570560
  97.2 13.1 %copy-start.5 = (f32[1,5120]{1,0:T(1,128)S(1)}, f32[1,5120]{1,0:T(1,128)}, u32[]{:S(2)}) copy-start(f32[1,5120]{1,0:T(1,128)} %param.9) | copy-start | bytes 61444
  108.2 2.1 copy-start.1
  110.3 2.1 copy-start.3
  129.2 115.6 %copy-start.2 = (bf16[1,180,320]{2,1,0:T(8,128)(2,1)S(1)}, bf16[1,180,320]{2,1,0:T(8,128)(2,1)}, u32[]{:S(2)}) copy-start(bf16[1,180,320]{2,1,0:T(8,128)(2,1)} %param.8) | copy-start | bytes 345604
  129.2 157.0 %copy-start.4 = (bf16[1,180,320]{2,1,0:T(8,128)(2,1)S(1)}, bf16[1,180,320]{2,1,0:T(8,128)(2,1)}, u32[]{:S(2)}) copy-start(bf16[1,180,320]{2,1,0:T(8,128)(2,1)} %param.13) | copy-start | bytes 345604
  129.3 215.4 %all-gather.7.cloned.1.call-start = ((), (), s32[]{:S(2)}) async-start(), calls=%async_computation.3 | async-start | bytes 2402304 | tf_op jit(solution)/shard_map/all_gather | solution.py:46
  287.1 122.0 %all-reduce.2.cloned.1.call-start = ((), (), s32[]{:S(2)}) async-start(), calls=%async_computation.1 | async-start | bytes 376832 | tf_op jit(solution)/shard_map/psum | solution.py:57
  347.9 4.5 %copy-start.6 = (s32[180]{0:T(256)S(1)}, s32[180]{0:T(256)}, u32[]{:S(2)}) copy-start(s32[180]{0:T(256)} %param.15) | copy-start | bytes 2164
Sparse Core Ops, SparseCore 0:
  10.1 87.0 all-gather.4
  129.4 114.3 reduce-scatter.3
  287.3 57.3 all-gather.6
  395.2 13.8 all-reduce.1
where the time goes:
time: 418 us; the launch traced here: 417 us
  waiting for transfers between devices  274 us (66%)
  blocking collectives  80.5 us (19%)
  local copies, waits for them, and re-layouts  29.3 us (7%)
  matrix products  15.9 us (4%)
  between operations  13.2 us (3%)
    unnamed x5, waiting for transfers between devices  114 us
    all_gather x1, waiting for transfers between devices, on_device(): whole_input = lax.all_gather(input_local, 'shard', axis=1, tiled=True)  88.6 us
    all_gather x1, waiting for transfers between devices, on_device(): lax.all_gather(grad_share, 'shard', axis=1, tiled=True)  57.4 us
    psum x1, blocking collectives, on_device(): proj = lax.psum(partial_proj, 'shard')[:, None] / width  41.3 us
    psum x1, blocking collectives, on_device(): current = lax.psum(own_local, 'shard')  39.2 us
    unnamed x19, local copies, waits for them, and re-layouts  14.9 us
    psum x1, waiting for transfers between devices, on_device(): delta = lax.psum(scores - current[:, None], 'member')  14.1 us
    all_gather x1, local copies, waits for them, and re-layouts, on_device(): whole_input = lax.all_gather(input_local, 'shard', axis=1, tiled=True)  11 us
  transfers between devices with their start and end apart: 4, of which 4 were waited for; matrix products, arithmetic and copies ran while one was open for 0% of the time, Pallas kernels for 0%

commit v1 on v0

--- a/solution.py
+++ b/solution.py
@@ -53,7 +53,7 @@
     entries = first_entry + lax.broadcasted_iota(jnp.int32, (1, vocab_local), 1)
     own_mask = (suffix_ids[:, None] == entries).astype(jnp.float32)
     own_local = jnp.sum(scores * own_mask, axis=1)
-    current = lax.psum(own_local, "shard")
+    current = jnp.sum(lax.all_gather(own_local, "shard"), axis=0)
     delta = lax.psum(scores - current[:, None], "member")
     return delta
 

time: 418 us -> 453 us (1.084)
  blocking collectives: 80.5 us -> 115 us
    unnamed x0 -> x1, blocking collectives: none -> 74.2 us
    psum x1 -> x0, blocking collectives: 39.2 us -> none  [on_device(): current = lax.psum(own_local, 'shard')]
    unnamed x19 -> x24, local copies, waits for them, and re-layouts: 14.9 us -> 15.9 us
where the time goes in v1:
time: 453 us
  waiting for transfers between devices  273 us (60%)
  blocking collectives  115 us (25%)
  local copies, waits for them, and re-layouts  30.3 us (7%)
  matrix products  15.9 us (4%)
  between operations  13.9 us (3%)
    unnamed x5, waiting for transfers between devices  114 us
    all_gather x1, waiting for transfers between devices, on_device(): whole_input = lax.all_gather(input_local, 'shard', axis=1, tiled=True)  88.6 us
    unnamed x1, blocking collectives  74.2 us
    all_gather x1, waiting for transfers between devices, on_device(): lax.all_gather(grad_share, 'shard', axis=1, tiled=True)  56 us
    psum x1, blocking collectives, on_device(): proj = lax.psum(partial_proj, 'shard')[:, None] / width  41.3 us
    unnamed x24, local copies, waits for them, and re-layouts  15.9 us
    psum x1, waiting for transfers between devices, on_device(): delta = lax.psum(scores - current[:, None], 'member')  14 us
    all_gather x1, local copies, waits for them, and re-layouts, on_device(): whole_input = lax.all_gather(input_local, 'shard', axis=1, tiled=True)  11 us
  transfers between devices with their start and end apart: 4, of which 4 were waited for; matrix products, arithmetic and copies ran while one was open for 0% of the time, Pallas kernels for 0%

profile of v1, /device:TPU:0, one launch (start us, length us, event | category | flops | bytes accessed | tf_op | source)
XLA Modules:
  0.0 452.7 jit_solution(8464161942415167688)
XLA Ops:
  6.5 0.0 copy-start
  6.5 0.0 all-gather.6.cloned.1.call-start
  6.5 2.0 copy.15
  8.5 0.0 all-gather.6.cloned.1.call-update
  8.6 0.0 reduce-scatter.4.cloned.1.call-start
  8.6 88.6 %all-gather.6.cloned.1.call-done = bf16[1,180,5120]{1,0,2:T(2,128)(2,1)} async-done(((bf16[1,180,320]{1,0,2:T(2,128)(2,1)}), bf16[1,180,5120]{1,0,2:T(2,128)(2,1)}) %all-gather.6.cloned.1.call-update) | async-done | bytes 1843216 | tf_op jit(solution)/shard_map/all_gather | solution.py:14
  97.2 0.0 copy-start.5
  97.2 11.0 %copy.16 = bf16[1,180,5120]{2,1,0:T(8,128)(2,1)} copy(bf16[1,180,5120]{1,0,2:T(2,128)(2,1)} %all-gather.6.cloned.1.call-done) | data formatting | bytes 3686400 | tf_op jit(solution)/shard_map/all_gather | solution.py:14
  108.2 0.0 copy-start.1
  108.2 2.1 fusion.1
  110.3 0.0 copy-done.5
  110.3 0.0 copy-done.1
  110.3 0.0 copy-start.3
  110.3 2.1 fusion.8
  112.4 0.0 copy-done.3
  112.5 6.2 %fusion.6 = f32[180,5120]{1,0:T(8,128)} fusion(bf16[1,5120,112]{1,2,0:T(8,128)(2,1)} %param.10, bf16[1,5120,112]{1,2,0:T(8,128)(2,1)} %param.11, bf16[1,180,5120]{2,1,0:T(8,128)(2,1)} %copy.16, f32[5120]{0:T(1024)S(1)} %bitcast.69, f32[180]{0:T(256)S(1)} %get-tuple-element.6, f32[180,112]{1,0:T(8,128)S(1)} %fusion.8, bf16[1,180,112]{2,1,0:T(8,128)(2,1)S(1)} %copy-done.3), kind=kOutput, calls=%fused_computation.9 | convolution fusion | flops 416784960 | bytes 7965520 | tf_op jit(solution)/shard_map/dot_general | solution.py:29
  118.7 4.9 %fusion = f32[5120,180]{0,1:T(8,128)} fusion(f32[180,5120]{1,0:T(8,128)} %fusion.6, bf16[1,5120,112]{1,2,0:T(8,128)(2,1)} %param.11, f32[180,112]{1,0:T(8,128)S(1)} %fusion.8, bf16[1,180,112]{2,1,0:T(8,128)(2,1)S(1)} %copy-done.3), kind=kOutput, calls=%fused_computation.1 | convolution fusion | flops 207501120 | bytes 8640640 | tf_op jit(solution)/shard_map/dot_general | solution.py:31
  123.6 5.6 %copy.18 = f32[5120,180]{1,0:T(8,128)} copy(f32[5120,180]{0,1:T(8,128)} %fusion) | data formatting | bytes 7372800
  129.2 0.0 copy-start.2
  129.2 0.0 copy-start.4
  129.2 0.0 reduce-scatter.4.cloned.1.call-update
  129.3 0.0 copy-start.7
  129.3 0.0 all-gather.8.cloned.1.call-start
  129.3 0.1 dynamic-slice_reduce_fusion
  129.4 114.3 %reduce-scatter.4.cloned.1.call-done = f32[320,180]{1,0:T(8,128)} async-done(((f32[5120,180]{1,0:T(8,128)}), f32[320,180]{1,0:T(8,128)}) %reduce-scatter.4.cloned.1.call-update) | async-done | bytes 230416
  243.7 1.1 copy.19
  244.9 0.0 copy-done.2
  244.9 0.1 fusion.33
  245.0 41.3 %psum.14 = f32[180]{0:T(256)S(1)} all-reduce(f32[180]{0:T(256)S(1)} %fusion.33), channel_id=1, replica_groups=mesh['member'=2,'shard'=16] {'shard'}, use_global_device_ids=true, to_apply=%region_3.0 | all-reduce | flops 180 | bytes 1440 | tf_op jit(solution)/shard_map/psum | solution.py:42
  286.3 0.0 copy-done.4
  286.3 0.8 fusion.34
  287.1 0.0 all-gather.8.cloned.1.call-update
  287.1 0.0 all-reduce.3.cloned.1.call-start
  287.2 0.0 copy-done.7
  287.2 0.7 dynamic-slice.1
  288.6 56.0 %all-gather.8.cloned.1.call-done = bf16[16,320,180]{1,2,0:T(8,128)(2,1)} async-done(((bf16[1,320,180]{1,2,0:T(8,128)(2,1)}), bf16[16,320,180]{1,2,0:T(8,128)(2,1)}) %all-gather.8.cloned.1.call-update) | async-done | bytes 1843216 | tf_op jit(solution)/shard_map/all_gather | solution.py:46
  344.6 3.3 copy.17
  347.9 4.5 %reshape.39 = bf16[5120,180]{0,1:T(8,128)(2,1)} reshape(bf16[16,320,180]{1,0,2:T(8,128)(2,1)} %copy.17) | data formatting | bytes 3686400
  352.4 0.0 copy-done
  352.4 0.0 copy-done.6
  352.4 2.6 select_reduce_fusion
  355.1 0.3 dynamic-update-slice
  355.4 74.2 %all-reduce = f32[2880]{0:T(1024)S(1)} all-reduce(f32[2880]{0:T(1024)S(1)} %dynamic-update-slice), channel_id=3, replica_groups=mesh['member'=2,'shard'=16] {'shard'}, use_global_device_ids=true, to_apply=%add | all-reduce | flops 2880 | bytes 23040
  429.6 0.1 reshape.32
  429.7 0.8 broadcast_subtract_fusion
  430.5 0.0 all-reduce.3.cloned.1.call-update
  430.5 14.0 %all-reduce.3.cloned.1.call-done = f32[180,256]{1,0:T(8,128)} async-done(((f32[180,256]{1,0:T(8,128)}), f32[180,256]{1,0:T(8,128)}) %all-reduce.3.cloned.1.call-update) | async-done | bytes 184336 | tf_op jit(solution)/shard_map/psum | solution.py:57
  444.6 1.6 copy.22
  (6 shorter events, 0.0 us)
Async XLA Ops:
  6.5 345.9 %copy-start = (bf16[1,256,5120]{2,1,0:T(8,128)(2,1)S(1)}, bf16[1,256,5120]{2,1,0:T(8,128)(2,1)}, u32[]{:S(2)}) copy-start(bf16[1,256,5120]{2,1,0:T(8,128)(2,1)} %param.14) | copy-start | bytes 7864324
  6.5 90.6 %all-gather.6.cloned.1.call-start = ((), (), s32[]{:S(2)}) async-start(), calls=%async_computation.2 | async-start | bytes 5570560 | tf_op jit(solution)/shard_map/all_gather | solution.py:14
  8.6 235.2 %reduce-scatter.4.cloned.1.call-start = ((), (), s32[]{:S(2)}) async-start(), calls=%async_computation.4 | async-start | bytes 5570560
  97.2 13.1 %copy-start.5 = (f32[1,5120]{1,0:T(1,128)S(1)}, f32[1,5120]{1,0:T(1,128)}, u32[]{:S(2)}) copy-start(f32[1,5120]{1,0:T(1,128)} %param.9) | copy-start | bytes 61444
  108.2 2.1 copy-start.1
  110.3 2.1 copy-start.3
  129.2 115.6 %copy-start.2 = (bf16[1,180,320]{2,1,0:T(8,128)(2,1)S(1)}, bf16[1,180,320]{2,1,0:T(8,128)(2,1)}, u32[]{:S(2)}) copy-start(bf16[1,180,320]{2,1,0:T(8,128)(2,1)} %param.8) | copy-start | bytes 345604
  129.2 157.0 %copy-start.4 = (bf16[1,180,320]{2,1,0:T(8,128)(2,1)S(1)}, bf16[1,180,320]{2,1,0:T(8,128)(2,1)}, u32[]{:S(2)}) copy-start(bf16[1,180,320]{2,1,0:T(8,128)(2,1)} %param.13) | copy-start | bytes 345604
  129.3 157.9 %copy-start.7 = (u32[32]{0:T(128)S(1)}, u32[32]{0:T(128)}, u32[]{:S(2)}) copy-start(u32[32]{0:T(128)} %constant.34) | copy-start | bytes 388
  129.3 215.3 %all-gather.8.cloned.1.call-start = ((), (), s32[]{:S(2)}) async-start(), calls=%async_computation.3 | async-start | bytes 2402304 | tf_op jit(solution)/shard_map/all_gather | solution.py:46
  287.1 157.4 %all-reduce.3.cloned.1.call-start = ((), (), s32[]{:S(2)}) async-start(), calls=%async_computation.1 | async-start | bytes 376832 | tf_op jit(solution)/shard_map/psum | solution.py:57
  347.9 4.5 %copy-start.6 = (s32[180]{0:T(256)S(1)}, s32[180]{0:T(256)}, u32[]{:S(2)}) copy-start(s32[180]{0:T(256)} %param.15) | copy-start | bytes 2164
Sparse Core Ops, SparseCore 0:
  10.1 87.0 all-gather.5
  129.4 114.3 reduce-scatter.3
  287.3 57.3 all-gather.7
  430.6 13.8 all-reduce.2
